TPU v7x, 512 devices: a whole 4x8x8 slice. The times are simulated.
512 devices in a mesh: left: 16 (over x, y_hi, core), right: 32 (over y_lo, z).
Axes of the slice: x: 4, y: 8 (y_hi: 2, y_lo: 4; y = y_hi * 4 + y_lo), z: 8, core: 2. Of those that a mesh axis runs over, the one named last changes fastest.
Arguments:
- left_table: bfloat16 [32768, 256], P('left'), may hold values from -1.5 to 1.5
- right_table: bfloat16 [16, 16384, 256], P('left', 'right'), may hold values from -1.5 to 1.5
- relations: float32 [512, 256], replicated, may hold values from -6 to 6
- source_ids: int32 [16, 32, 1024], P('left', 'right'), may hold values from 0 to 2047
- relation_ids: int32 [16, 32, 1024], P('left', 'right'), may hold values from 0 to 511
- target_ids: int32 [16, 32, 1024], P('left', 'right'), may hold values from 0 to 511
- negative_ids: int32 [16, 32, 1, 1024], P('left', 'right'), may hold values from 0 to 511
- edge_counts: int32 [16, 32], P('left', 'right'), may hold values from 1 to 1024
Outputs:
- left_next: bfloat16 [32768, 256], P('left')
- right_next: bfloat16 [16, 16384, 256], P('left', 'right')
- relations_next: float32 [512, 256], replicated
Inputs may be any that keep to these rules, and one draw needn't show every extreme that they name: Edge slots at positions from edge_counts to 1023 hold ids but are padding.
All inputs are finite; a program needn't handle non-finite values.
Results may differ from a plain program's by a relative error of at most 0.0013.
Values may be sent and summed in bfloat16 or wider, within the bound.
No kernel may reach another device: no remote copies, remote signals or barrier semaphores. Data moves between devices by JAX's collectives and lax.ppermute only.
A program may use at most 64 MiB of HBM per device.

v0:
```python
import jax
import jax.numpy as jnp
from jax import lax
from jax.sharding import PartitionSpec as P

step_size = 0.5
relation_step = 12.0


def passed_along(array, axis, by):
    peers = lax.axis_size(axis)
    return lax.ppermute(array, axis, [(i, (i + by) % peers) for i in range(peers)])


def block_terms(left_blk, right_blk, relations, src, kind, dst, neg, live):
    half = relations.shape[1] // 2
    head = jnp.take(left_blk, src, axis=0).astype(jnp.float32)
    tail = jnp.take(right_blk, dst, axis=0).astype(jnp.float32)
    rel = jnp.take(relations, kind, axis=0)
    hre, him = (head[:, :half], head[:, half:])
    rre, rim = (rel[:, :half], rel[:, half:])
    query = jnp.concatenate([hre * rre - him * rim, hre * rim + him * rre], axis=1)
    q_low = query.astype(jnp.bfloat16)
    pos = jnp.sum(query * tail, axis=1)
    negrows = jnp.take(right_blk, neg, axis=0)
    scores = lax.dot_general(
        q_low, negrows, (((1,), (1,)), ((), ())), preferred_element_type=jnp.float32
    )
    c_pos = -jax.nn.sigmoid(-pos) * live
    c_neg = (jax.nn.sigmoid(scores) * (live[:, None] / neg.shape[0])).astype(jnp.bfloat16)
    g_query = jnp.dot(c_neg, negrows, preferred_element_type=jnp.float32) + c_pos[:, None] * tail
    g_neg = lax.dot_general(
        c_neg, q_low, (((0,), (0,)), ((), ())), preferred_element_type=jnp.float32
    )
    g_tail = c_pos[:, None] * query
    gre, gim = (g_query[:, :half], g_query[:, half:])
    grad_h = jnp.concatenate([gre * rre + gim * rim, -gre * rim + gim * rre], axis=1)
    grad_r = jnp.concatenate([gre * hre + gim * him, -gre * him + gim * hre], axis=1)
    return (grad_h, grad_r, g_tail, g_neg)


def shards(
    left_table,
    right_table,
    relations,
    source_ids,
    relation_ids,
    target_ids,
    negative_ids,
    edge_counts,
):
    right_blk = right_table[0]
    src_all = source_ids[0, 0]
    kind_all = relation_ids[0, 0]
    dst_all = target_ids[0, 0]
    negs = negative_ids[0, 0]
    count = edge_counts[0, 0]
    blocks = negs.shape[0]
    width = src_all.shape[0] // blocks
    live_blocks = (count + width - 1) // width

    def one(index, carry):
        lgrad, rgrad, tgrad = carry
        start = index * width
        n = lax.dynamic_index_in_dim(negs, index, 0, keepdims=False)
        live = (start + jnp.arange(width, dtype=jnp.int32) < count).astype(jnp.float32)
        grad_h, grad_r, g_tail, g_neg = block_terms(
            left_table, right_blk, relations, src_all, kind_all, dst_all, n, live
        )
        lgrad = lgrad.at[src_all].add(grad_h)
        rgrad = rgrad.at[kind_all].add(grad_r)
        tgrad = tgrad.at[dst_all].add(g_tail).at[n].add(g_neg)
        return (lgrad, rgrad, tgrad)

    init = (
        jnp.zeros(left_table.shape, jnp.float32),
        jnp.zeros(relations.shape, jnp.float32),
        jnp.zeros(right_blk.shape, jnp.float32),
    )
    left_grad, rel_grad, right_grad = lax.fori_loop(0, live_blocks, one, init)
    updated = (right_blk.astype(jnp.float32) - step_size * right_grad).astype(jnp.bfloat16)
    moved = passed_along(updated, "right", 1)
    left_total = lax.psum(left_grad, "right")
    rel_total = lax.psum(rel_grad, ("left", "right"))
    left_next = (left_table.astype(jnp.float32) - step_size * left_total).astype(jnp.bfloat16)
    relations_next = relations - relation_step * rel_total
    return (left_next, moved[None], relations_next)


def solution(mesh):
    return jax.shard_map(
        shards,
        mesh=mesh,
        in_specs=(
            P("left", None),
            P("left", "right", None),
            P(),
            P("left", "right", None),
            P("left", "right", None),
            P("left", "right", None),
            P("left", "right", None, None),
            P("left", "right"),
        ),
        out_specs=(P("left", None), P("left", "right", None), P()),
        check_vma=False,
    )
```

profile of v0, /device:TPU:2, one launch (start us, length us, event | category | flops | bytes accessed | tf_op | source)
XLA Modules:
  0.0 709.8 jit_solution(15141002125790694229)
XLA Ops:
  7.2 0.0 all-reduce.5.cloned.1.call-start
  7.9 0.7 compare_and_fusion.4
  8.6 0.7 fusion.13
  9.2 0.7 compare_select_fusion.9
  9.9 0.7 compare_and_fusion.6
  10.6 0.7 compare_select_fusion.8
  11.3 0.7 compare_and_fusion.5
  12.0 0.0 copy-start
  12.0 4.9 gather_fusion.4
  16.9 0.0 copy-start.1
  16.9 3.9 gather_fusion.6
  20.9 0.2 select_convert_fusion.1
  21.1 3.5 gather_fusion.5
  24.6 0.2 broadcast_select_fusion.4
  24.8 0.1 multiply_subtract_fusion.2
  24.9 0.0 copy-start.3
  24.9 0.0 copy-start.10
  24.9 0.0 copy-start.11
  25.0 0.0 copy-start.12
  25.0 0.0 copy-start.13
  25.0 0.4 fusion.12
  25.5 1.4 broadcast_in_dim.66
  26.9 80.2 %while.17 = (s32[]{:T(128)}, f32[2048,256]{1,0:T(8,128)}, f32[512,256]{1,0:T(8,128)S(1)}, f32[512,256]{1,0:T(8,128)S(1)}, s32[]{:T(128)}, /*index=5*/s32[1024]{0...) while((s32[]{:T(128)}, f32[2048,256]{1,0:T(8,128)}, ...), condition=%wide.region_6.8_spmd, body=%wide.region_1.7_spmd.sunk | while | flops 1624953856 | bytes 75646288 | solution.py:80
  27.3 0.7 negate_select_fusion.2
  28.0 5.0 gather_fusion
  32.9 3.9 gather_fusion.3
  36.9 1.0 copy.28
  37.9 5.0 gather_fusion.2
  42.9 1.2 copy.27
  44.1 1.0 select_convert_fusion.3
  45.2 4.7 gather_fusion.1
  49.8 2.6 copy.26
  52.4 1.4 broadcast_select_fusion.10
  53.8 0.1 copy-done.4
  54.0 0.2 multiply_subtract_fusion.4
  54.2 0.8 copy-done.5
  55.0 0.8 copy-done.6
  55.8 1.1 fusion.30
  56.9 2.5 copy.31
  59.4 6.7 scatter_fusion.2
  66.2 0.0 copy-start.9
  66.2 3.0 multiply_convert_fusion.2
  69.2 1.8 convolution_add_fusion.2
  71.0 1.8 fusion.31
  72.8 6.7 scatter_fusion.3
  79.5 3.0 multiply_add_fusion.7
  82.6 1.0 pad_maximum_fusion.5
  83.6 2.5 copy.29
  86.1 9.4 %scatter_fusion = f32[2048,256]{1,0:T(8,128)} fusion(f32[2048,256]{1,0:T(8,128)} %get-tuple-element.393, s32[1024]{0:T(1024)S(1)} %bitcast.59, f32[1024,256]{1,0:T(8,128)} %copy.29), kind=kCustom, calls=%fused_computation.7.clone.1 | custom fusion | flops 262144 | bytes 3149824 | tf_op jit(solution)/shard_map/while/body/scatter-add | solution.py:70
  95.5 2.1 pad_maximum_fusion.6
  97.6 2.5 copy.30
  100.1 6.7 scatter_fusion.1
  107.1 0.0 copy-start.2
  107.1 0.8 copy-done.2
  107.9 0.0 all-reduce.5.cloned.1.call-update
  107.9 0.0 all-reduce.3.cloned.1.call-start
  108.0 0.7 all-reduce.3.cloned.1.call-update
  108.7 0.1 subtract_convert_fusion.1
  108.8 4.3 collective-permute-start
  113.0 270.8 %all-reduce.5.cloned.1.call-done = f32[512,256]{1,0:T(8,128)} async-done(((f32[512,256]{1,0:T(8,128)}), f32[512,256]{1,0:T(8,128)}) %all-reduce.5.cloned.1.call-update) | async-done | bytes 524304 | tf_op jit(solution)/shard_map/psum | solution.py:84
  383.8 1.9 multiply_subtract_fusion.1
  385.7 313.7 %all-reduce.3.cloned.1.call-done = f32[2048,256]{1,0:T(8,128)} async-done(((f32[2048,256]{1,0:T(8,128)}), f32[2048,256]{1,0:T(8,128)}) %all-reduce.3.cloned.1.call-update) | async-done | bytes 2097168 | tf_op jit(solution)/shard_map/psum | solution.py:83
  699.4 2.8 subtract_convert_fusion
  702.2 0.7 copy.54
  (32 shorter events, 0.2 us)
Async XLA Ops:
  7.2 376.7 %all-reduce.5.cloned.1.call-start = ((), (), s32[]{:S(2)}) async-start(), calls=%async_computation.1 | async-start | bytes 1048576 | tf_op jit(solution)/shard_map/psum | solution.py:84
  12.0 4.9 copy-start
  16.9 4.2 copy-start.1
  24.9 2.0 copy-start.3
  24.9 2.0 copy-start.10
  24.9 2.0 copy-start.11
  25.0 2.0 copy-start.12
  25.0 2.0 copy-start.13
  52.4 1.5 copy-start.4
  54.0 1.0 copy-start.5
  55.0 0.8 copy-start.6
  66.2 3.0 copy-start.8
  66.2 3.0 copy-start.9
  69.2 1.8 copy-start.7
  107.1 0.8 copy-start.2
  107.9 591.5 %all-reduce.3.cloned.1.call-start = ((), (), s32[]{:S(2)}) async-start(), calls=%async_computation | async-start | bytes 4194304 | tf_op jit(solution)/shard_map/psum | solution.py:83
  108.8 277.0 %collective-permute-start = (bf16[512,256]{1,0:T(8,128)(2,1)S(1)}, bf16[512,256]{1,0:T(8,128)(2,1)S(1)}, u32[]{:S(2)}, u32[]{:S(2)}) collective-permute-start(bf16[512,256]{1,0:T(8,128)(2,1)S(1)} %subtract_convert_fusion.1), channel_id=1, source_target_pairs={{0,1},{1,2},{2,3},{3,4},{4,5},{5,6},{6,7},{7,8},{8,9},{9,10},{10,1... | collective-permute-start | bytes 786440 | tf_op jit(solution)/shard_map/ppermute | solution.py:12
Sparse Core Ops, SparseCore 0:
  108.1 275.7 all-reduce.4
  386.7 312.6 all-reduce.2
where the time goes:
time: 711 us; the launch traced here: 710 us
  waiting for transfers between devices  585 us (82%)
  other arithmetic  50.1 us (7%)
  local copies, waits for them, and re-layouts  48.1 us (7%)
  between operations  14.9 us (2%)
    psum x1, waiting for transfers between devices, shards(): left_total = lax.psum(left_grad, 'right')  314 us
    psum x1, waiting for transfers between devices, shards(): rel_total = lax.psum(rel_grad, ('left', 'right'))  271 us
  transfers between devices with their start and end apart: 3, of which 2 were waited for; matrix products, arithmetic and copies ran while one was open for 0% of the time, Pallas kernels for 0%

commit v1 on v0

--- a/solution.py
+++ b/solution.py
@@ -5,6 +5,7 @@
 
 step_size = 0.5
 relation_step = 12.0
+read_plate_over_axis = lambda values: lax.psum(lax.psum(values, "right"), "left")
 
 
 def passed_along(array, axis, by):
@@ -81,7 +82,7 @@
     updated = (right_blk.astype(jnp.float32) - step_size * right_grad).astype(jnp.bfloat16)
     moved = passed_along(updated, "right", 1)
     left_total = lax.psum(left_grad, "right")
-    rel_total = lax.psum(rel_grad, ("left", "right"))
+    rel_total = read_plate_over_axis(rel_grad)
     left_next = (left_table.astype(jnp.float32) - step_size * left_total).astype(jnp.bfloat16)
     relations_next = relations - relation_step * rel_total
     return (left_next, moved[None], relations_next)

time: 711 us -> 623 us (0.88)
  the two profiles are of different devices: /device:TPU:2 before, /device:TPU:1 now
where the time goes in v1:
time: 623 us; the launch traced here: 622 us
  waiting for transfers between devices  497 us (80%)
  other arithmetic  50.1 us (8%)
  local copies, waits for them, and re-layouts  48.1 us (8%)
  between operations  14.9 us (2%)
  matrix products  6.52 us (1%)
    psum x1, waiting for transfers between devices, shards(): left_total = lax.psum(left_grad, 'right')  280 us
    psum x1, waiting for transfers between devices, lax.psum(lax.psum(values, 'right'), 'left')  202 us
    ppermute x1, waiting for transfers between devices, passed_along(): lax.ppermute(array, axis, [(i, (i + by) % peers) for i in range(peers)])  15.7 us
    scatter-add x2, other arithmetic, one(): tgrad = tgrad.at[dst_all].add(g_tail).at[n].add(g_neg)  13.5 us
  transfers between devices with their start and end apart: 3, of which 3 were waited for; matrix products, arithmetic and copies ran while one was open for 0% of the time, Pallas kernels for 0%

profile of v1, /device:TPU:1, one launch (start us, length us, event | category | flops | bytes accessed | tf_op | source)
XLA Modules:
  0.0 622.0 jit_solution(6471389901041582001)
XLA Ops:
  7.2 0.0 all-reduce.6.cloned.1.call-start
  7.9 0.7 compare_and_fusion.4
  8.6 0.7 fusion.13
  9.2 0.7 compare_select_fusion.9
  9.9 0.7 compare_and_fusion.6
  10.6 0.7 compare_select_fusion.8
  11.3 0.7 compare_and_fusion.5
  12.0 0.0 copy-start
  12.0 4.9 gather_fusion.4
  16.9 0.0 copy-start.1
  16.9 3.9 gather_fusion.6
  20.9 0.2 select_convert_fusion.1
  21.1 3.5 gather_fusion.5
  24.6 0.2 broadcast_select_fusion.4
  24.8 0.1 multiply_subtract_fusion.2
  24.9 0.0 copy-start.3
  24.9 0.0 copy-start.10
  24.9 0.0 copy-start.11
  25.0 0.0 copy-start.12
  25.0 0.4 fusion.12
  25.5 1.4 broadcast_in_dim.66
  26.9 80.1 %while.17 = (s32[]{:T(128)}, f32[2048,256]{1,0:T(8,128)}, f32[512,256]{1,0:T(8,128)S(1)}, f32[512,256]{1,0:T(8,128)S(1)}, s32[]{:T(128)}, /*index=5*/s32[1024]{0...) while((s32[]{:T(128)}, f32[2048,256]{1,0:T(8,128)}, ...), condition=%wide.region_6.8_spmd, body=%wide.region_1.7_spmd.sunk | while | flops 1624953856 | bytes 75646288 | solution.py:81
  27.3 0.7 negate_select_fusion.2
  27.9 5.0 gather_fusion
  32.9 3.9 gather_fusion.3
  36.9 1.0 copy.28
  37.9 5.0 gather_fusion.2
  42.9 1.2 copy.27
  44.1 1.0 select_convert_fusion.3
  45.2 4.7 gather_fusion.1
  49.9 2.6 copy.26
  52.4 1.4 broadcast_select_fusion.10
  53.8 0.1 copy-done.4
  54.0 0.2 multiply_subtract_fusion.4
  54.2 0.8 copy-done.5
  55.0 0.8 copy-done.6
  55.8 1.1 fusion.30
  56.9 2.5 copy.31
  59.4 6.7 %scatter_fusion.2 = f32[512,256]{1,0:T(8,128)S(1)} fusion(f32[512,256]{1,0:T(8,128)S(1)} %get-tuple-element.397, s32[1024]{0:T(1024)S(1)} %bitcast.70, f32[1024,256]{1,0:T(8,128)} %copy.31), kind=kCustom, calls=%fused_computation.9.clone.1 | custom fusion | flops 262144 | bytes 3149824 | tf_op jit(solution)/shard_map/while/body/scatter-add | solution.py:73
  66.2 0.0 copy-start.9
  66.2 3.0 multiply_convert_fusion.2
  69.2 1.8 convolution_add_fusion.2
  71.0 1.7 fusion.31
  72.7 6.7 %scatter_fusion.3 = f32[512,256]{1,0:T(8,128)S(1)} fusion(f32[512,256]{1,0:T(8,128)S(1)} %scatter_fusion.2, s32[1024]{0:T(1024)S(1)} %bitcast.69, f32[1024,256]{1,0:T(8,128)} %fusion.31), kind=kCustom, calls=%fused_computation.10.clone.1 | custom fusion | flops 262144 | bytes 3149824 | tf_op jit(solution)/shard_map/while/body/scatter-add | solution.py:73
  79.5 3.0 multiply_add_fusion.7
  82.5 1.0 pad_maximum_fusion.5
  83.5 2.5 copy.29
  86.1 9.4 %scatter_fusion = f32[2048,256]{1,0:T(8,128)} fusion(f32[2048,256]{1,0:T(8,128)} %get-tuple-element.395, s32[1024]{0:T(1024)S(1)} %bitcast.59, f32[1024,256]{1,0:T(8,128)} %copy.29), kind=kCustom, calls=%fused_computation.7.clone.1 | custom fusion | flops 262144 | bytes 3149824 | tf_op jit(solution)/shard_map/while/body/scatter-add | solution.py:71
  95.4 2.1 pad_maximum_fusion.6
  97.5 2.5 copy.30
  100.1 6.7 %scatter_fusion.1 = f32[512,256]{1,0:T(8,128)S(1)} fusion(f32[512,256]{1,0:T(8,128)S(1)} %get-tuple-element.396, s32[1024]{0:T(1024)S(1)} %bitcast.57, f32[1024,256]{1,0:T(8,128)} %copy.30), kind=kCustom, calls=%fused_computation.8.clone.1 | custom fusion | flops 262144 | bytes 3149824 | tf_op jit(solution)/shard_map/while/body/scatter-add | solution.py:72
  107.1 0.0 copy-start.2
  107.1 0.8 copy-done.2
  107.8 0.0 all-reduce.6.cloned.1.call-update
  107.9 0.0 all-reduce.4.cloned.1.call-start
  107.9 0.1 subtract_convert_fusion.1
  108.0 4.8 collective-permute-start
  112.8 15.7 %collective-permute-done = bf16[512,256]{1,0:T(8,128)(2,1)S(1)} collective-permute-done((bf16[512,256]{1,0:T(8,128)(2,1)S(1)}, bf16[512,256]{1,0:T(8,128)(2,1)S(1)}, u32[]{:S(2)}, u32[]{:S(2)}) %collective-permute-start) | collective-permute-done | bytes 262176 | tf_op jit(solution)/shard_map/ppermute | solution.py:13
  128.5 279.6 %all-reduce.6.cloned.1.call-done = (f32[2048,256]{1,0:T(8,128)}, f32[512,256]{1,0:T(8,128)}) async-done(((f32[2048,256]{1,0:T(8,128)}, f32[512,256]{1,0:T(8,128)}), (f32[2048,256]{1,0:T(8,128)}, f32[512,256]{1,0:T(8,128)})) %all-reduce.6.cloned.1.call-update) | async-done | bytes 2621456 | tf_op jit(solution)/shard_map/psum | solution.py:84
  408.1 0.0 all-reduce.4.cloned.1.call-update
  408.1 2.8 subtract_convert_fusion
  410.9 201.6 %all-reduce.4.cloned.1.call-done = f32[512,256]{1,0:T(8,128)} async-done(((f32[512,256]{1,0:T(8,128)}), f32[512,256]{1,0:T(8,128)}) %all-reduce.4.cloned.1.call-update) | async-done | bytes 524304 | tf_op jit(solution)/shard_map/psum | solution.py:8
  612.5 1.9 multiply_subtract_fusion.1
  614.4 0.7 copy.55
  (32 shorter events, 0.2 us)
Async XLA Ops:
  7.2 400.9 %all-reduce.6.cloned.1.call-start = ((), (), s32[]{:S(2)}) async-start(), calls=%async_computation.1 | async-start | bytes 5242880 | tf_op jit(solution)/shard_map/psum | solution.py:84
  12.0 4.9 copy-start
  16.9 4.2 copy-start.1
  24.9 2.0 copy-start.3
  24.9 2.0 copy-start.10
  24.9 2.0 copy-start.11
  25.0 2.0 copy-start.12
  25.0 2.0 copy-start.13
  52.4 1.5 copy-start.4
  54.0 1.0 copy-start.5
  55.0 0.8 copy-start.6
  66.2 3.0 copy-start.8
  66.2 3.0 copy-start.9
  69.2 1.8 copy-start.7
  107.1 0.8 copy-start.2
  107.9 504.7 %all-reduce.4.cloned.1.call-start = ((), (), s32[]{:S(2)}) async-start(), calls=%async_computation | async-start | bytes 1048576 | tf_op jit(solution)/shard_map/psum | solution.py:8
  108.0 20.5 %collective-permute-start = (bf16[512,256]{1,0:T(8,128)(2,1)S(1)}, bf16[512,256]{1,0:T(8,128)(2,1)S(1)}, u32[]{:S(2)}, u32[]{:S(2)}) collective-permute-start(bf16[512,256]{1,0:T(8,128)(2,1)S(1)} %subtract_convert_fusion.1), channel_id=1, source_target_pairs={{0,1},{1,2},{2,3},{3,4},{4,5},{5,6},{6,7},{7,8},{8,9},{9,10},{10,1... | collective-permute-start | bytes 786440 | tf_op jit(solution)/shard_map/ppermute | solution.py:13
Sparse Core Ops, SparseCore 0:
  108.0 300.0 all-reduce.5
  411.0 201.5 all-reduce.3
